TPU v7x, 32 devices: a whole 2x2x4 slice. The times are simulated.
32 devices in a mesh: dp: 8 (over z, y), mp: 4 (over x, core).
Axes of the slice: x: 2, y: 2, z: 4, core: 2. Of those that a mesh axis runs over, the one named last changes fastest.
Arguments:
- hidden: bfloat16 [16384, 768], P('dp'), may hold values from -6 to 6
- upstream: bfloat16 [16384, 768], P('dp'), may hold values from -3 to 3
- segment_ids: int32 [16384], P('dp'), may hold values from 0 to 16, as said below
- cls_positions: int32 [16, 16], P('dp'), may hold values from 0 to 872, as said below
- positives: int32 [128], replicated, may hold values from 0 to 127, each once
- w_query: bfloat16 [768, 768], P(None, 'mp'), may hold values from -0.21875 to 0.21875
- b_query: float32 [768], P('mp'), may hold values from -3 to 3
- w_key: bfloat16 [768, 768], P(None, 'mp'), may hold values from -0.21875 to 0.21875
- w_value: bfloat16 [768, 768], P(None, 'mp'), may hold values from -0.21875 to 0.21875
- b_value: float32 [768], P('mp'), may hold values from -3 to 3
- w_out: bfloat16 [768, 768], P('mp'), may hold values from -1.25 to 1.25
- b_out: float32 [768], replicated, may hold values from -2.5 to 2.5
- gain_attn: float32 [768], replicated, may hold values from 0.5 to 1.5
- shift_attn: float32 [768], replicated, may hold values from -2.5 to 2.5
- w_inner: bfloat16 [768, 3072], P(None, 'mp'), may hold values from -0.21875 to 0.21875
- b_inner: float32 [3072], P('mp'), may hold values from -3 to 3
- w_outer: bfloat16 [3072, 768], P('mp'), may hold values from -0.109375 to 0.109375
- b_outer: float32 [768], replicated, may hold values from -2.5 to 2.5
- gain_final: float32 [768], replicated, may hold values from 0.5 to 1.5
- shift_final: float32 [768], replicated, may hold values from -2.5 to 2.5
Outputs:
- mean_loss: float32 [1], replicated
- layer_out: bfloat16 [16384, 768], P('dp')
- grad_hidden: float32 [16384, 768], P('dp')
- grad_w_query: float32 [768, 768], P(None, 'mp')
- grad_b_query: float32 [768], P('mp')
- grad_w_key: float32 [768, 768], P(None, 'mp')
- grad_w_value: float32 [768, 768], P(None, 'mp')
- grad_b_value: float32 [768], P('mp')
- grad_w_out: float32 [768, 768], P('mp')
- grad_b_out: float32 [768], replicated
- grad_gain_attn: float32 [768], replicated
- grad_shift_attn: float32 [768], replicated
- grad_w_inner: float32 [768, 3072], P(None, 'mp')
- grad_b_inner: float32 [3072], P('mp')
- grad_w_outer: float32 [3072, 768], P('mp')
- grad_b_outer: float32 [768], replicated
- grad_gain_final: float32 [768], replicated
- grad_shift_final: float32 [768], replicated
Inputs may be any that keep to these rules, and one draw needn't show every extreme that they name: `segment_ids`: each packed row of 1024 tokens holds 16 consecutive segments numbered 0 to 15 in order, even numbers queries and odd numbers passages, then padding tokens numbered 2 * 8, of which every row has some. `cls_positions`: entry j < 8 of row r is the first position within the row of segment 2 j, entry 8 + j that of segment 2 j + 1, as given by segment_ids. `positives`: every passage is the positive of exactly one query.
All inputs are finite; a program needn't handle non-finite values.
Results may differ from a plain program's by a relative error of at most 0.013.
Values may be sent and summed in bfloat16 or wider, within the bound.
A program may use at most 128 MiB of HBM per device.

v0:
```python
from functools import partial
import math
import jax
import jax.numpy as jnp
from jax import lax
from jax.sharding import PartitionSpec as P

D = 768
HEAD_DIM = 64
LEN = 1024
PAIRS = 8


def contract_rows(left_arr, right_arr):
    return lax.dot_general(
        left_arr, right_arr, (((0,), (0,)), ((), ())), preferred_element_type=jnp.float32
    )


def contract_cols(left_arr, right_arr):
    return lax.dot_general(
        left_arr, right_arr, (((1,), (1,)), ((), ())), preferred_element_type=jnp.float32
    )


def norm_forward(summed, gain_vec, offset_vec):
    centre = summed - jnp.mean(summed, axis=-1, keepdims=True)
    inverse = lax.rsqrt(jnp.mean(centre * centre, axis=-1, keepdims=True) + 1e-12)
    normed = centre * inverse
    return (normed * gain_vec + offset_vec, normed, inverse)


def norm_backward(grad_rows, normed, inverse, gain_vec):
    scaled = grad_rows * gain_vec
    grad_in = inverse * (
        scaled
        - jnp.mean(scaled, axis=-1, keepdims=True)
        - normed * jnp.mean(scaled * normed, axis=-1, keepdims=True)
    )
    return (grad_in, jnp.sum(grad_rows * normed, axis=0), jnp.sum(grad_rows, axis=0))


def soft_rows(logits, targets, logit_scale):
    largest = jnp.max(logits, axis=-1, keepdims=True)
    expo_rows = jnp.exp(logits - largest)
    totals = jnp.sum(expo_rows, axis=-1, keepdims=True)
    target_hit = targets[:, None] == jnp.arange(logits.shape[1], dtype=jnp.int32)[None, :]
    cross_ent = (
        largest[:, 0] + jnp.log(totals[:, 0]) - jnp.sum(jnp.where(target_hit, logits, 0.0), axis=-1)
    )
    logit_grad = (expo_rows / totals - target_hit.astype(jnp.float32)) * logit_scale
    return (cross_ent, logit_grad)


def on_device(
    hidden,
    upstream,
    segment_ids,
    cls_positions,
    positives,
    w_query,
    b_query,
    w_key,
    w_value,
    b_value,
    w_out,
    b_out,
    gain_attn,
    shift_attn,
    w_inner,
    b_inner,
    w_outer,
    b_outer,
    gain_final,
    shift_final,
):
    highest = lax.Precision.HIGHEST
    token_count = hidden.shape[0]
    row_count = token_count // LEN
    local_width = w_query.shape[1]
    head_count = local_width // HEAD_DIM
    head_scale = 1.0 / math.sqrt(HEAD_DIM)
    logit_scale = 3.0 / math.sqrt(D)
    block_rows = min(512, LEN)
    per_row = LEN // block_rows
    block_count = token_count // block_rows
    query_rows = (
        (jnp.dot(hidden, w_query, preferred_element_type=jnp.float32) + b_query) * head_scale
    ).astype(jnp.bfloat16)
    key_rows = jnp.dot(hidden, w_key, preferred_element_type=jnp.float32).astype(jnp.bfloat16)
    value_rows = (jnp.dot(hidden, w_value, preferred_element_type=jnp.float32) + b_value).astype(
        jnp.bfloat16
    )
    query_blocks = query_rows.reshape(block_count, block_rows, head_count, HEAD_DIM)
    key_seqs = key_rows.reshape(row_count, LEN, head_count, HEAD_DIM)
    value_seqs = value_rows.reshape(row_count, LEN, head_count, HEAD_DIM)
    segment_blocks = segment_ids.reshape(block_count, block_rows)
    segment_seqs = segment_ids.reshape(row_count, LEN)

    def block_scores(block_index):
        row_index = block_index // per_row
        query_block = query_blocks[block_index]
        key_block = key_seqs[row_index]
        scores = jnp.einsum(
            "qhd,khd->hqk", query_block, key_block, preferred_element_type=jnp.float32
        )
        same_doc = segment_blocks[block_index][:, None] == segment_seqs[row_index][None, :]
        return (jnp.where(same_doc[None, :, :], scores, -1e30), row_index, query_block, key_block)

    def forward_block(block_index):
        scores, row_index, query_block, key_block = block_scores(block_index)
        largest = jnp.max(scores, axis=-1, keepdims=True)
        expo_rows = jnp.exp(scores - largest)
        totals = jnp.sum(expo_rows, axis=-1, keepdims=True)
        weights = (expo_rows / totals).astype(jnp.bfloat16)
        context_block = jnp.einsum(
            "hqk,khd->qhd", weights, value_seqs[row_index], preferred_element_type=jnp.float32
        )
        return (context_block.astype(jnp.bfloat16), largest + jnp.log(totals))

    context_blocks, log_totals = lax.map(forward_block, jnp.arange(block_count))
    context = context_blocks.reshape(token_count, local_width)
    attention_part = lax.psum(jnp.dot(context, w_out, preferred_element_type=jnp.float32), "mp")
    attention_part = attention_part + b_out
    hidden_part = hidden.astype(jnp.float32)
    middle_part, normed_one, inverse_one = norm_forward(
        hidden_part + attention_part, gain_attn, shift_attn
    )
    middle_low_part = middle_part.astype(jnp.bfloat16)
    pre_act = jnp.dot(middle_low_part, w_inner, preferred_element_type=jnp.float32) + b_inner
    activated, gelu_back = jax.vjp(partial(jax.nn.gelu, approximate=False), pre_act)
    inner_act = activated.astype(jnp.bfloat16)
    feed_part = lax.psum(jnp.dot(inner_act, w_outer, preferred_element_type=jnp.float32), "mp")
    feed_part = feed_part + b_outer
    final_part, normed_two, inverse_two = norm_forward(
        middle_part + feed_part, gain_final, shift_final
    )
    out_part = final_part.astype(jnp.bfloat16)
    own_count = row_count * PAIRS
    row_start = jnp.arange(row_count, dtype=jnp.int32)[:, None] * LEN
    cls_index = jnp.concatenate(
        [
            (row_start + cls_positions[:, :PAIRS]).reshape(-1),
            (row_start + cls_positions[:, PAIRS:]).reshape(-1),
        ]
    )
    selector = cls_index[:, None] == jnp.arange(token_count, dtype=jnp.int32)[None, :]
    picked = jnp.dot(
        selector.astype(jnp.bfloat16), out_part, preferred_element_type=jnp.float32
    ).astype(jnp.bfloat16)
    query_vecs = picked[:own_count]
    passage_vecs = picked[own_count:]
    device = lax.axis_index("dp")
    dp_count = lax.axis_size("dp")
    own_positive = lax.dynamic_slice_in_dim(positives, device * own_count, own_count)
    passage_all = lax.all_gather(passage_vecs, "dp", axis=0, tiled=True)
    logits = contract_cols(query_vecs, passage_all) * logit_scale
    cross_ent, logit_grad = soft_rows(logits, own_positive, logit_scale)
    loss_term = jnp.sum(cross_ent)
    grad_query_vecs = jnp.dot(logit_grad, passage_all.astype(jnp.float32), precision=highest)
    passage_terms = lax.dot_general(
        logit_grad, query_vecs.astype(jnp.float32), (((0,), (0,)), ((), ())), precision=highest
    )
    grad_passage_vecs = lax.psum_scatter(passage_terms, "dp", scatter_dimension=0, tiled=True)
    grad_cls = jnp.concatenate([grad_query_vecs, grad_passage_vecs], axis=0)
    selector_part = selector.astype(jnp.float32)
    grad_final_part = upstream.astype(jnp.float32) + lax.dot_general(
        selector_part, grad_cls, (((0,), (0,)), ((), ())), precision=highest
    )
    grad_two_part, grad_gain_final, grad_shift_final = norm_backward(
        grad_final_part, normed_two, inverse_two, gain_final
    )
    grad_feed_part = grad_two_part.astype(jnp.bfloat16)
    grad_b_outer = jnp.sum(grad_feed_part.astype(jnp.float32), axis=0)
    grad_w_outer = contract_rows(inner_act, grad_feed_part)
    grad_inner = contract_cols(grad_feed_part, w_outer)
    grad_pre = gelu_back(grad_inner)[0].astype(jnp.bfloat16)
    grad_b_inner = jnp.sum(grad_pre.astype(jnp.float32), axis=0)
    grad_w_inner = contract_rows(middle_low_part, grad_pre)
    back_part = lax.psum(contract_cols(grad_pre, w_inner), "mp")
    grad_middle_part = grad_two_part + back_part
    grad_one_part, grad_gain_attn, grad_shift_attn = norm_backward(
        grad_middle_part, normed_one, inverse_one, gain_attn
    )
    grad_attn_part = grad_one_part.astype(jnp.bfloat16)
    grad_b_out = jnp.sum(grad_attn_part.astype(jnp.float32), axis=0)
    grad_w_out = contract_rows(context, grad_attn_part)
    grad_context = contract_cols(grad_attn_part, w_out).astype(jnp.bfloat16)
    grad_context_blocks = grad_context.reshape(block_count, block_rows, head_count, HEAD_DIM)

    def backward_block(carried, block_index):
        grad_keys, grad_values = carried
        scores, row_index, query_block, key_block = block_scores(block_index)
        probs_full = jnp.exp(scores - log_totals[block_index])
        weights = probs_full.astype(jnp.bfloat16)
        grad_ctx_block = grad_context_blocks[block_index]
        grad_probs = jnp.einsum(
            "qhd,khd->hqk",
            grad_ctx_block,
            value_seqs[row_index],
            preferred_element_type=jnp.float32,
        )
        centre = jnp.sum(probs_full * grad_probs, axis=-1, keepdims=True)
        grad_scores = (probs_full * (grad_probs - centre)).astype(jnp.bfloat16)
        grad_query_block = jnp.einsum(
            "hqk,khd->qhd", grad_scores, key_block, preferred_element_type=jnp.float32
        )
        key_update = jnp.einsum(
            "hqk,qhd->khd", grad_scores, query_block, preferred_element_type=jnp.float32
        )
        value_update = jnp.einsum(
            "hqk,qhd->khd", weights, grad_ctx_block, preferred_element_type=jnp.float32
        )
        grad_keys = grad_keys.at[row_index].add(key_update.reshape(LEN, local_width))
        grad_values = grad_values.at[row_index].add(value_update.reshape(LEN, local_width))
        return ((grad_keys, grad_values), grad_query_block.reshape(block_rows, local_width))

    zero_seqs = jnp.zeros((row_count, LEN, local_width), jnp.float32)
    (grad_keys, grad_values), grad_query_blocks = lax.scan(
        backward_block, (zero_seqs, zero_seqs), jnp.arange(block_count)
    )
    grad_query_pre = grad_query_blocks.reshape(token_count, local_width).astype(
        jnp.bfloat16
    ) * jnp.bfloat16(head_scale)
    grad_key_low = grad_keys.reshape(token_count, local_width).astype(jnp.bfloat16)
    grad_value_low = grad_values.reshape(token_count, local_width).astype(jnp.bfloat16)
    grad_w_query = contract_rows(hidden, grad_query_pre)
    grad_b_query = jnp.sum(grad_query_pre.astype(jnp.float32), axis=0)
    grad_w_key = contract_rows(hidden, grad_key_low)
    grad_w_value = contract_rows(hidden, grad_value_low)
    grad_b_value = jnp.sum(grad_value_low.astype(jnp.float32), axis=0)
    input_part = (
        contract_cols(grad_query_pre, w_query)
        + contract_cols(grad_key_low, w_key)
        + contract_cols(grad_value_low, w_value)
    )
    gain_parts = jnp.stack([grad_gain_attn, grad_shift_attn, grad_gain_final, grad_shift_final])
    gain_term = jnp.where(lax.axis_index("mp") == 0, gain_parts, 0.0)
    hidden_sum, gain_sum = lax.psum((input_part, gain_term), "mp")
    grad_hidden = grad_one_part + hidden_sum
    every_sum = lax.psum(
        (
            grad_w_query,
            grad_b_query,
            grad_w_key,
            grad_w_value,
            grad_b_value,
            grad_w_out,
            grad_b_out,
            gain_sum,
            grad_w_inner,
            grad_b_inner,
            grad_w_outer,
            grad_b_outer,
            loss_term,
        ),
        "dp",
    )
    gains_done = every_sum[7]
    mean_loss = every_sum[12] / (dp_count * own_count)
    return (
        mean_loss.reshape(1),
        out_part,
        grad_hidden,
        every_sum[0],
        every_sum[1],
        every_sum[2],
        every_sum[3],
        every_sum[4],
        every_sum[5],
        every_sum[6],
        gains_done[0],
        gains_done[1],
        every_sum[8],
        every_sum[9],
        every_sum[10],
        every_sum[11],
        gains_done[2],
        gains_done[3],
    )


def solution(mesh):
    return jax.shard_map(
        on_device,
        mesh=mesh,
        in_specs=(
            P("dp", None),
            P("dp", None),
            P("dp"),
            P("dp", None),
            P(),
            P(None, "mp"),
            P("mp"),
            P(None, "mp"),
            P(None, "mp"),
            P("mp"),
            P("mp", None),
            P(),
            P(),
            P(),
            P(None, "mp"),
            P("mp"),
            P("mp", None),
            P(),
            P(),
            P(),
        ),
        out_specs=(
            P(),
            P("dp", None),
            P("dp", None),
            P(None, "mp"),
            P("mp"),
            P(None, "mp"),
            P(None, "mp"),
            P("mp"),
            P("mp", None),
            P(),
            P(),
            P(),
            P(None, "mp"),
            P("mp"),
            P("mp", None),
            P(),
            P(),
            P(),
        ),
        check_vma=False,
    )
```

profile of v0, /device:TPU:0, one launch (start us, length us, event | category | flops | bytes accessed | tf_op | source)
XLA Modules:
  0.0 1092.0 jit_solution(5726283432003561547)
XLA Ops:
  8.8 3.2 fusion.55
  12.7 3.2 fusion.56
  17.5 3.1 convolution_convert_fusion.1
  21.4 47.4 %while.32 = (s32[]{:T(128)}, bf16[4,512,3,64]{1,3,2,0:T(8,128)(2,1)}, f32[4,3,512,1]{2,1,3,0:T(4,128)}, s32[4]{0:T(128)S(1)}, bf16[2,1024,3,64]{1,3,2,0:T(8,128)...) while((s32[]{:T(128)}, ...), condition=%wide.region_3.4_spmd, body=%wide.region_0.3_spmd.sunk | while | flops 417430016 | bytes 22226292 | solution.py:121
  30.7 2.6 fusion.143
  66.2 2.6 fusion.143
  71.9 3.7 fusion.82
  75.9 122.2 %all-reduce.8.cloned.1.call-done = f32[2048,768]{1,0:T(8,128)} async-done(((f32[2048,768]{1,0:T(8,128)}), f32[2048,768]{1,0:T(8,128)}) %all-reduce.8.cloned.1.call-update) | async-done | bytes 6291472 | tf_op jit(solution)/shard_map/psum | solution.py:123
  198.1 4.6 fusion.80
  205.4 18.3 %multiply_convert_fusion.1 = (bf16[2048,768]{1,0:T(8,128)(2,1)S(1)}, f32[2048,768]{1,0:T(8,128)}, f32[2048,768]{1,0:T(8,128)}) fusion(f32[768]{0:T(1024)S(1)} %copy-done.48, bf16[2048,768]{1,0:T(8,128)(2,1)S(1)} %fusion.53, bf16[768,768]{1,0:T(8,128)(2,1)S(1)} %copy-done), kind=kOutput, calls=%fused_computation.81 | convolution fusion | flops 2519728128 | bytes 20057088 | tf_op jit(solution)/shard_map/dot_general | solution.py:130
  225.5 4.5 fusion.83
  231.0 118.9 %all-reduce.10.cloned.1.call-done = f32[2048,768]{1,0:T(8,128)} async-done(((f32[2048,768]{1,0:T(8,128)}), f32[2048,768]{1,0:T(8,128)}) %all-reduce.10.cloned.1.call-update) | async-done | bytes 6291472 | tf_op jit(solution)/shard_map/psum | solution.py:133
  349.9 5.7 fusion.78
  360.0 30.8 %all_gather.3 = bf16[128,768]{1,0:T(8,128)(2,1)S(1)} all-gather(bf16[16,768]{1,0:T(8,128)(2,1)S(1)} %slice.71), channel_id=1, replica_groups=mesh['dp'=8,'mp'=4] {'dp'}, dimensions={0}, use_global_device_ids=true | all-gather | bytes 221184 | tf_op jit(solution)/shard_map/all_gather | solution.py:156
  393.5 61.2 %reduce-scatter.2.cloned.1.call-done = f32[16,768]{1,0:T(8,128)} async-done(((f32[128,768]{1,0:T(8,128)}), f32[16,768]{1,0:T(8,128)}) %reduce-scatter.2.cloned.1.call-update) | async-done | bytes 49168 | tf_op jit(solution)/shard_map/reduce_scatter | solution.py:164
  454.7 8.7 multiply_reduce_fusion.1
  463.4 5.3 convert_reduce_fusion
  468.8 9.5 convert_reduce_fusion.1
  480.0 4.5 fusion.84
  485.0 118.3 %all-reduce.12.cloned.1.call-done = f32[2048,768]{1,0:T(8,128)} async-done(((f32[2048,768]{1,0:T(8,128)}), f32[2048,768]{1,0:T(8,128)}) %all-reduce.12.cloned.1.call-update) | async-done | bytes 6291472 | tf_op jit(solution)/shard_map/psum | solution.py:180
  603.3 8.7 multiply_reduce_fusion.2
  612.1 5.2 convert_reduce_fusion.2
  617.2 2.7 copy-done.3
  624.3 75.6 %while.33 = (s32[]{:T(128)}, f32[2,1024,192]{1,2,0:T(8,128)S(1)}, f32[2,1024,192]{1,2,0:T(8,128)}, bf16[4,512,192]{1,2,0:T(8,128)(2,1)}, s32[4]{0:T(128)S(1)}, /...) while((s32[]{:T(128)}, f32[2,1024,192]{1,2,0:T(8,128)S(1)}, ...), condition=%wide.region_24.25_spmd, body=%wide.region_21.24_spmd.sunk | while | flops 1026816512 | bytes 77071920 | solution.py:219
  705.3 3.7 add_add_fusion
  709.2 7.1 fusion.87
  716.2 7.1 fusion.70
  730.9 12.2 %psum.138 = f32[4,768]{1,0:T(4,128)S(1)} all-reduce(f32[4,768]{1,0:T(4,128)S(1)} %maximum_select_fusion), channel_id=1, replica_groups=mesh['dp'=8,'mp'=4] {'mp'}, use_global_device_ids=true, to_apply=%region_40.41 | all-reduce | flops 3072 | bytes 24576 | tf_op jit(solution)/shard_map/psum | solution.py:239
  744.5 37.9 %all-reduce = (f32[]{:T(128)}, f32[192]{0:T(256)}, f32[192]{0:T(256)}, f32[768]{0:T(1024)}, f32[4,768]{1,0:T(4,128)S(1)}, /*index=5*/f32[768]{0:T(1024)}, f32[768]{0:T(1024)}) all-reduce(f32[]{:T(128)} %subtract_reduce_fusion, f32[192]{0:T(256)S(1)} %convert_reduce_fusion.4, ...), channel_id=1, replica_groups=mesh['dp'=8,'mp'=4] {'dp'}, use_global_device_ids=true, to_apply=%region_14.15 | all-reduce | flops 5761 | bytes 46088 | tf_op jit(solution)/shard_map/psum | solution.py:241
  783.7 45.6 %all-reduce.14.cloned.1.call-done = f32[2048,768]{1,0:T(8,128)} async-done(((f32[2048,768]{1,0:T(8,128)}), f32[2048,768]{1,0:T(8,128)}) %all-reduce.14.cloned.1.call-update) | async-done | bytes 6291472 | tf_op jit(solution)/shard_map/psum | solution.py:239
  829.3 8.1 add.272
  837.4 235.7 %all-reduce.16.cloned.1.call-done = (f32[768,192]{0,1:T(8,128)}, f32[768,192]{0,1:T(8,128)}, f32[768,192]{0,1:T(8,128)}, f32[192,768]{1,0:T(8,128)}, f32[768,768]{1,0:T(8,128)}, /*index=5*/f32[768,768]{1,0:T(8,128)}) async-done(((f32[768,192]{0,1:T(8,128)}, f32[768,192]{0,1:T(8,128)}, f32[768,192]{0,1:T(8,128)}, f32[192,768]{1,0:T(8,128)}, f32[768,768]{1,0:T(8,128)}, /*index=5*/f32[768,768]{1,0:T(8,128)}), ...) | async-done | bytes 7077904 | tf_op jit(solution)/shard_map/psum | solution.py:241
  (302 shorter events, 138.4 us)
Async XLA Ops:
  7.2 198.2 %copy-start = (bf16[768,768]{1,0:T(8,128)(2,1)S(1)}, bf16[768,768]{1,0:T(8,128)(2,1)}, u32[]{:S(2)}) copy-start(bf16[768,768]{1,0:T(8,128)(2,1)} %param.42) | copy-start | bytes 3538948
  7.2 190.9 %all-reduce.8.cloned.1.call-start = ((), (), s32[]{:S(2)}) async-start(), calls=%async_computation.1 | async-start | bytes 12582912 | tf_op jit(solution)/shard_map/psum | solution.py:123
  21.4 50.6 %copy-start.22 = (bf16[192,768]{1,0:T(8,128)(2,1)S(1)}, bf16[192,768]{1,0:T(8,128)(2,1)}, u32[]{:S(2)}) copy-start(bf16[192,768]{1,0:T(8,128)(2,1)} %param.38) | copy-start | bytes 884740
  68.8 6.9 copy-start.10
  71.9 126.2 %copy-start.43 = (f32[768]{0:T(1024)S(1)}, f32[768]{0:T(1024)}, u32[]{:S(2)}) copy-start(f32[768]{0:T(1024)} %param.39) | copy-start | bytes 9220
  75.7 274.2 %all-reduce.10.cloned.1.call-start = ((), (), s32[]{:S(2)}) async-start(), calls=%async_computation.2 | async-start | bytes 12582912 | tf_op jit(solution)/shard_map/psum | solution.py:133
  205.4 18.3 %copy-start.17 = (bf16[2048,768]{1,0:T(8,128)(2,1)}, bf16[2048,768]{1,0:T(8,128)(2,1)S(1)}, u32[]{:S(2)}) copy-start(bf16[2048,768]{1,0:T(8,128)(2,1)S(1)} %fusion.53) | copy-start | bytes 9437188
  205.4 20.1 %copy-start.46 = (bf16[768,768]{1,0:T(8,128)(2,1)S(1)}, bf16[768,768]{1,0:T(8,128)(2,1)}, u32[]{:S(2)}) copy-start(bf16[768,768]{1,0:T(8,128)(2,1)} %param.44) | copy-start | bytes 3538948
  230.0 120.0 %copy-start.44 = (f32[768]{0:T(1024)S(1)}, f32[768]{0:T(1024)}, u32[]{:S(2)}) copy-start(f32[768]{0:T(1024)} %param.45) | copy-start | bytes 9220
  230.0 224.7 %reduce-scatter.2.cloned.1.call-start = ((), (), s32[]{:S(2)}) async-start(), calls=%async_computation.3 | async-start | bytes 442368 | tf_op jit(solution)/shard_map/reduce_scatter | solution.py:164
  391.0 72.4 %copy-start.34 = (f32[16]{0:T(128)}, f32[16]{0:T(128)S(1)}, u32[]{:S(2)}) copy-start(f32[16]{0:T(128)S(1)} %get-tuple-element.447) | copy-start | bytes 196
  391.7 71.7 %copy-start.36 = (f32[16]{0:T(128)}, f32[16]{0:T(128)S(1)}, u32[]{:S(2)}) copy-start(f32[16]{0:T(128)S(1)} %get-tuple-element.368) | copy-start | bytes 196
  393.0 210.4 %all-reduce.12.cloned.1.call-start = ((), (), s32[]{:S(2)}) async-start(), calls=%async_computation.4 | async-start | bytes 12582912 | tf_op jit(solution)/shard_map/psum | solution.py:180
  454.7 14.1 %slice-start.2 = ((s8[6291456]{0:T(1024)(128)(4,1)}), s8[4194304]{0:T(1024)(128)(4,1)S(1)}, s32[]{:S(2)}) async-start(s8[6291456]{0:T(1024)(128)(4,1)} %bitcast.195), calls=%async_computation.9 | async-start | bytes 8388608
  463.4 5.4 copy-start.47
  463.4 5.4 slice-start.3
  468.8 9.5 copy-start.5
  484.6 344.7 %all-reduce.14.cloned.1.call-start = ((), (), s32[]{:S(2)}) async-start(), calls=%async_computation.5 | async-start | bytes 12582912 | tf_op jit(solution)/shard_map/psum | solution.py:239
  619.9 4.4 copy-start.33
  636.1 4.2 copy-start.7
  709.1 364.0 %all-reduce.16.cloned.1.call-start = ((), (), s32[]{:S(2)}) async-start(), calls=%async_computation.6 | async-start | bytes 14155776 | tf_op jit(solution)/shard_map/psum | solution.py:241
  709.2 7.1 copy-start.19
  716.2 7.1 copy-start.6
  716.2 7.1 copy-start.16
  723.4 5.0 slice-start
  723.4 5.0 copy-start.13
  728.4 16.1 %copy-start.30 = (f32[768]{0:T(1024)S(1)}, f32[768]{0:T(1024)}, u32[]{:S(2)}) copy-start(f32[768]{0:T(1024)} %get-tuple-element.425) | copy-start | bytes 9220
  728.4 16.1 %copy-start.31 = (f32[768]{0:T(1024)S(1)}, f32[768]{0:T(1024)}, u32[]{:S(2)}) copy-start(f32[768]{0:T(1024)} %get-tuple-element.427) | copy-start | bytes 9220
  728.5 16.1 %copy-start.42 = (f32[768]{0:T(1024)S(1)}, f32[768]{0:T(1024)}, u32[]{:S(2)}) copy-start(f32[768]{0:T(1024)} %get-tuple-element.450) | copy-start | bytes 9220
  1073.1 7.9 copy-start.21
  1073.1 9.3 copy-start.20
  1073.1 10.7 copy-start.1
  (41 other events, 91.4 us)
Sparse Core Ops, SparseCore 0:
  75.8 122.2 all-reduce.7
  230.1 119.7 all-reduce.9
  393.1 61.5 reduce-scatter.1
  484.7 118.5 all-reduce.11
  709.2 120.0 all-reduce.13
  835.4 237.6 all-reduce.15
where the time goes:
time: 1100 us; the launch traced here: 1090 us
  waiting for transfers between devices  702 us (64%)
  matrix products  144 us (13%)
  blocking collectives  80.9 us (7%)
  other arithmetic  73 us (7%)
  local copies, waits for them, and re-layouts  42.4 us (4%)
  loops' own time  31.8 us (3%)
  between operations  16.8 us (2%)
    psum x1, waiting for transfers between devices, on_device(): lax.psum((grad_w_query, grad_b_query, grad_w_key, grad_w_value, grad_b_va...  236 us
    psum x1, waiting for transfers between devices, on_device(): lax.psum(jnp.dot(context, w_out, preferred_element_type=jnp.float32), 'mp')  122 us
    psum x1, waiting for transfers between devices, on_device(): lax.psum(jnp.dot(inner_act, w_outer, preferred_element_type=jnp.float32),...  119 us
    psum x1, waiting for transfers between devices, on_device(): back_part = lax.psum(contract_cols(grad_pre, w_inner), 'mp')  118 us
    reduce_scatter x1, waiting for transfers between devices, on_device(): lax.psum_scatter(passage_terms, 'dp', scatter_dimension=0, tiled=True)  61.2 us
    psum x1, waiting for transfers between devices, on_device(): hidden_sum, gain_sum = lax.psum((input_part, gain_term), 'mp')  45.6 us
    psum x1, blocking collectives, on_device(): lax.psum((grad_w_query, grad_b_query, grad_w_key, grad_w_value, grad_b_va...  37.9 us
    all_gather x1, blocking collectives, on_device(): passage_all = lax.all_gather(passage_vecs, 'dp', axis=0, tiled=True)  30.8 us
  transfers between devices with their start and end apart: 6, of which 6 were waited for; matrix products, arithmetic and copies ran while one was open for 3% of the time, Pallas kernels for 0%

commit v1 on v0

--- a/solution.py
+++ b/solution.py
@@ -130,7 +130,9 @@
     pre_act = jnp.dot(middle_low_part, w_inner, preferred_element_type=jnp.float32) + b_inner
     activated, gelu_back = jax.vjp(partial(jax.nn.gelu, approximate=False), pre_act)
     inner_act = activated.astype(jnp.bfloat16)
-    feed_part = lax.psum(jnp.dot(inner_act, w_outer, preferred_element_type=jnp.float32), "mp")
+    part = jnp.dot(inner_act, w_outer, preferred_element_type=jnp.float32)
+    parts = lax.all_gather(part, "mp")
+    feed_part = jnp.sum(parts, axis=0)
     feed_part = feed_part + b_outer
     final_part, normed_two, inverse_two = norm_forward(
         middle_part + feed_part, gain_final, shift_final

time: 1100 us -> 1150 us (1.045)
  waiting for transfers between devices: 702 us -> 737 us
  other arithmetic: 73 us -> 85.7 us
    all_gather x0 -> x1, waiting for transfers between devices: none -> 154 us  [on_device(): parts = lax.all_gather(part, 'mp')]
    psum x1 -> x0, waiting for transfers between devices: 119 us -> none  [on_device(): lax.psum(jnp.dot(inner_act, w_outer, preferred_element_type=jnp.float32),...]
    reduce_sum x0 -> x1, other arithmetic: none -> 12.6 us  [on_device(): feed_part = jnp.sum(parts, axis=0)]
where the time goes in v1:
time: 1150 us; the launch traced here: 1140 us
  waiting for transfers between devices  737 us (64%)
  matrix products  144 us (13%)
  other arithmetic  85.7 us (7%)
  blocking collectives  80.8 us (7%)
  local copies, waits for them, and re-layouts  42.3 us (4%)
  loops' own time  31.8 us (3%)
  between operations  16.8 us (1%)
    psum x1, waiting for transfers between devices, on_device(): lax.psum((grad_w_query, grad_b_query, grad_w_key, grad_w_value, grad_b_va...  236 us
    all_gather x1, waiting for transfers between devices, on_device(): parts = lax.all_gather(part, 'mp')  154 us
    psum x1, waiting for transfers between devices, on_device(): lax.psum(jnp.dot(context, w_out, preferred_element_type=jnp.float32), 'mp')  122 us
    psum x1, waiting for transfers between devices, on_device(): back_part = lax.psum(contract_cols(grad_pre, w_inner), 'mp')  118 us
    reduce_scatter x1, waiting for transfers between devices, on_device(): lax.psum_scatter(passage_terms, 'dp', scatter_dimension=0, tiled=True)  61 us
    psum x1, waiting for transfers between devices, on_device(): hidden_sum, gain_sum = lax.psum((input_part, gain_term), 'mp')  45.6 us
    psum x1, blocking collectives, on_device(): lax.psum((grad_w_query, grad_b_query, grad_w_key, grad_w_value, grad_b_va...  37.9 us
    all_gather x1, blocking collectives, on_device(): passage_all = lax.all_gather(passage_vecs, 'dp', axis=0, tiled=True)  30.7 us
  transfers between devices with their start and end apart: 6, of which 6 were waited for; matrix products, arithmetic and copies ran while one was open for 3% of the time, Pallas kernels for 0%

profile of v1, /device:TPU:0, one launch (start us, length us, event | category | flops | bytes accessed | tf_op | source)
XLA Modules:
  0.0 1139.5 jit_solution(14359836886609176762)
XLA Ops:
  8.8 3.2 fusion.55
  12.7 3.2 fusion.56
  17.5 3.1 convolution_convert_fusion.1
  21.4 47.4 %while.32 = (s32[]{:T(128)}, bf16[4,512,3,64]{1,3,2,0:T(8,128)(2,1)}, f32[4,3,512,1]{2,1,3,0:T(4,128)}, s32[4]{0:T(128)S(1)}, bf16[2,1024,3,64]{1,3,2,0:T(8,128)...) while((s32[]{:T(128)}, ...), condition=%wide.region_3.4_spmd, body=%wide.region_0.3_spmd.sunk | while | flops 417430016 | bytes 22226292 | solution.py:121
  66.2 2.6 fusion.143
  71.9 3.7 fusion.82
  75.9 122.2 %all-reduce.7.cloned.1.call-done = f32[2048,768]{1,0:T(8,128)} async-done(((f32[2048,768]{1,0:T(8,128)}), f32[2048,768]{1,0:T(8,128)}) %all-reduce.7.cloned.1.call-update) | async-done | bytes 6291472 | tf_op jit(solution)/shard_map/psum | solution.py:123
  198.1 4.6 fusion.80
  205.5 18.3 %multiply_convert_fusion.1 = (bf16[2048,768]{1,0:T(8,128)(2,1)S(1)}, f32[2048,768]{1,0:T(8,128)}, f32[2048,768]{1,0:T(8,128)}) fusion(f32[768]{0:T(1024)S(1)} %copy-done.48, bf16[2048,768]{1,0:T(8,128)(2,1)S(1)} %fusion.53, bf16[768,768]{1,0:T(8,128)(2,1)S(1)} %copy-done), kind=kOutput, calls=%fused_computation.81 | convolution fusion | flops 2519728128 | bytes 20057088 | tf_op jit(solution)/shard_map/dot_general | solution.py:130
  225.5 4.5 fusion.83
  231.0 154.2 %all-gather.3.cloned.1.call-done = f32[8192,768]{1,0:T(8,128)} async-done(((f32[2048,768]{1,0:T(8,128)}), f32[8192,768]{1,0:T(8,128)}) %all-gather.3.cloned.1.call-update) | async-done | bytes 25165840 | tf_op jit(solution)/shard_map/all_gather | solution.py:134
  385.2 12.6 %reduce_sum.215 = f32[2048,768]{1,0:T(8,128)} reduce(f32[4,2048,768]{2,1,0:T(8,128)} %bitcast.182, f32[]{:T(128)} %constant.234.clone.1), dimensions={0}, to_apply=%region_7.8 | reduce | flops 4718592 | bytes 31457284 | tf_op jit(solution)/shard_map/reduce_sum | solution.py:135
  397.8 5.7 fusion.78
  407.9 30.7 %all_gather.11 = bf16[128,768]{1,0:T(8,128)(2,1)S(1)} all-gather(bf16[16,768]{1,0:T(8,128)(2,1)S(1)} %slice.71), channel_id=1, replica_groups=mesh['dp'=8,'mp'=4] {'dp'}, dimensions={0}, use_global_device_ids=true | all-gather | bytes 221184 | tf_op jit(solution)/shard_map/all_gather | solution.py:158
  441.3 61.0 %reduce-scatter.2.cloned.1.call-done = f32[16,768]{1,0:T(8,128)} async-done(((f32[128,768]{1,0:T(8,128)}), f32[16,768]{1,0:T(8,128)}) %reduce-scatter.2.cloned.1.call-update) | async-done | bytes 49168 | tf_op jit(solution)/shard_map/reduce_scatter | solution.py:166
  502.3 8.7 multiply_reduce_fusion.1
  511.0 5.3 convert_reduce_fusion
  516.4 9.5 convert_reduce_fusion.1
  527.6 4.5 fusion.84
  532.6 118.3 %all-reduce.9.cloned.1.call-done = f32[2048,768]{1,0:T(8,128)} async-done(((f32[2048,768]{1,0:T(8,128)}), f32[2048,768]{1,0:T(8,128)}) %all-reduce.9.cloned.1.call-update) | async-done | bytes 6291472 | tf_op jit(solution)/shard_map/psum | solution.py:182
  650.9 8.7 multiply_reduce_fusion.2
  659.7 5.2 convert_reduce_fusion.2
  664.8 2.7 copy-done.3
  671.9 75.6 %while.33 = (s32[]{:T(128)}, f32[2,1024,192]{1,2,0:T(8,128)S(1)}, f32[2,1024,192]{1,2,0:T(8,128)}, bf16[4,512,192]{1,2,0:T(8,128)(2,1)}, s32[4]{0:T(128)S(1)}, /...) while((s32[]{:T(128)}, f32[2,1024,192]{1,2,0:T(8,128)S(1)}, ...), condition=%wide.region_24.25_spmd, body=%wide.region_21.24_spmd.sunk | while | flops 1026816512 | bytes 77071920 | solution.py:221
  752.9 3.7 add_add_fusion
  756.7 7.1 fusion.87
  763.8 7.1 fusion.70
  778.4 12.3 %psum.130 = f32[4,768]{1,0:T(4,128)S(1)} all-reduce(f32[4,768]{1,0:T(4,128)S(1)} %maximum_select_fusion), channel_id=1, replica_groups=mesh['dp'=8,'mp'=4] {'mp'}, use_global_device_ids=true, to_apply=%region_40.41 | all-reduce | flops 3072 | bytes 24576 | tf_op jit(solution)/shard_map/psum | solution.py:241
  792.1 37.9 %all-reduce = (f32[]{:T(128)}, f32[192]{0:T(256)}, f32[192]{0:T(256)}, f32[768]{0:T(1024)}, f32[4,768]{1,0:T(4,128)S(1)}, /*index=5*/f32[768]{0:T(1024)}, f32[768]{0:T(1024)}) all-reduce(f32[]{:T(128)} %subtract_reduce_fusion, f32[192]{0:T(256)S(1)} %convert_reduce_fusion.4, ...), channel_id=1, replica_groups=mesh['dp'=8,'mp'=4] {'dp'}, use_global_device_ids=true, to_apply=%region_14.15 | all-reduce | flops 5761 | bytes 46088 | tf_op jit(solution)/shard_map/psum | solution.py:243
  831.3 45.6 %all-reduce.11.cloned.1.call-done = f32[2048,768]{1,0:T(8,128)} async-done(((f32[2048,768]{1,0:T(8,128)}), f32[2048,768]{1,0:T(8,128)}) %all-reduce.11.cloned.1.call-update) | async-done | bytes 6291472 | tf_op jit(solution)/shard_map/psum | solution.py:241
  876.9 8.1 add.270
  885.0 235.6 %all-reduce.13.cloned.1.call-done = (f32[768,192]{0,1:T(8,128)}, f32[768,192]{0,1:T(8,128)}, f32[768,192]{0,1:T(8,128)}, f32[192,768]{1,0:T(8,128)}, f32[768,768]{1,0:T(8,128)}, /*index=5*/f32[768,768]{1,0:T(8,128)}) async-done(((f32[768,192]{0,1:T(8,128)}, f32[768,192]{0,1:T(8,128)}, f32[768,192]{0,1:T(8,128)}, f32[192,768]{1,0:T(8,128)}, f32[768,768]{1,0:T(8,128)}, /*index=5*/f32[768,768]{1,0:T(8,128)}), ...) | async-done | bytes 7077904 | tf_op jit(solution)/shard_map/psum | solution.py:243
  (303 shorter events, 140.9 us)
Async XLA Ops:
  7.2 198.3 %copy-start = (bf16[768,768]{1,0:T(8,128)(2,1)S(1)}, bf16[768,768]{1,0:T(8,128)(2,1)}, u32[]{:S(2)}) copy-start(bf16[768,768]{1,0:T(8,128)(2,1)} %param.42) | copy-start | bytes 3538948
  7.2 190.9 %all-reduce.7.cloned.1.call-start = ((), (), s32[]{:S(2)}) async-start(), calls=%async_computation.1 | async-start | bytes 12582912 | tf_op jit(solution)/shard_map/psum | solution.py:123
  21.4 50.6 %copy-start.22 = (bf16[192,768]{1,0:T(8,128)(2,1)S(1)}, bf16[192,768]{1,0:T(8,128)(2,1)}, u32[]{:S(2)}) copy-start(bf16[192,768]{1,0:T(8,128)(2,1)} %param.38) | copy-start | bytes 884740
  68.8 6.9 copy-start.10
  71.9 126.2 %copy-start.43 = (f32[768]{0:T(1024)S(1)}, f32[768]{0:T(1024)}, u32[]{:S(2)}) copy-start(f32[768]{0:T(1024)} %param.39) | copy-start | bytes 9220
  75.7 309.5 %all-gather.3.cloned.1.call-start = ((), (), s32[]{:S(2)}) async-start(), calls=%async_computation.5 | async-start | bytes 31457280 | tf_op jit(solution)/shard_map/all_gather | solution.py:134
  205.5 18.3 %copy-start.17 = (bf16[2048,768]{1,0:T(8,128)(2,1)}, bf16[2048,768]{1,0:T(8,128)(2,1)S(1)}, u32[]{:S(2)}) copy-start(bf16[2048,768]{1,0:T(8,128)(2,1)S(1)} %fusion.53) | copy-start | bytes 9437188
  205.5 20.0 %copy-start.46 = (bf16[768,768]{1,0:T(8,128)(2,1)S(1)}, bf16[768,768]{1,0:T(8,128)(2,1)}, u32[]{:S(2)}) copy-start(bf16[768,768]{1,0:T(8,128)(2,1)} %param.44) | copy-start | bytes 3538948
  230.0 272.3 %reduce-scatter.2.cloned.1.call-start = ((), (), s32[]{:S(2)}) async-start(), calls=%async_computation.2 | async-start | bytes 442368 | tf_op jit(solution)/shard_map/reduce_scatter | solution.py:166
  385.2 12.6 %copy-start.44 = (f32[768]{0:T(1024)S(1)}, f32[768]{0:T(1024)}, u32[]{:S(2)}) copy-start(f32[768]{0:T(1024)} %param.45) | copy-start | bytes 9220
  438.8 72.2 %copy-start.34 = (f32[16]{0:T(128)}, f32[16]{0:T(128)S(1)}, u32[]{:S(2)}) copy-start(f32[16]{0:T(128)S(1)} %get-tuple-element.447) | copy-start | bytes 196
  439.5 71.4 %copy-start.36 = (f32[16]{0:T(128)}, f32[16]{0:T(128)S(1)}, u32[]{:S(2)}) copy-start(f32[16]{0:T(128)S(1)} %get-tuple-element.368) | copy-start | bytes 196
  440.8 210.2 %all-reduce.9.cloned.1.call-start = ((), (), s32[]{:S(2)}) async-start(), calls=%async_computation.3 | async-start | bytes 12582912 | tf_op jit(solution)/shard_map/psum | solution.py:182
  502.3 14.1 %slice-start.2 = ((s8[6291456]{0:T(1024)(128)(4,1)}), s8[4194304]{0:T(1024)(128)(4,1)S(1)}, s32[]{:S(2)}) async-start(s8[6291456]{0:T(1024)(128)(4,1)} %bitcast.197), calls=%async_computation.9 | async-start | bytes 8388608
  511.0 5.4 copy-start.47
  511.0 5.4 slice-start.3
  516.3 9.5 copy-start.5
  532.1 344.8 %all-reduce.11.cloned.1.call-start = ((), (), s32[]{:S(2)}) async-start(), calls=%async_computation.4 | async-start | bytes 12582912 | tf_op jit(solution)/shard_map/psum | solution.py:241
  667.5 4.3 copy-start.33
  740.2 4.2 copy-start.7
  756.7 364.0 %all-reduce.13.cloned.1.call-start = ((), (), s32[]{:S(2)}) async-start(), calls=%async_computation.6 | async-start | bytes 14155776 | tf_op jit(solution)/shard_map/psum | solution.py:243
  756.7 7.1 copy-start.19
  763.8 7.1 copy-start.6
  763.8 7.1 copy-start.16
  770.9 5.0 slice-start
  770.9 5.0 copy-start.13
  776.0 16.1 %copy-start.30 = (f32[768]{0:T(1024)S(1)}, f32[768]{0:T(1024)}, u32[]{:S(2)}) copy-start(f32[768]{0:T(1024)} %get-tuple-element.425) | copy-start | bytes 9220
  776.0 16.1 %copy-start.31 = (f32[768]{0:T(1024)S(1)}, f32[768]{0:T(1024)}, u32[]{:S(2)}) copy-start(f32[768]{0:T(1024)} %get-tuple-element.427) | copy-start | bytes 9220
  776.0 16.1 %copy-start.42 = (f32[768]{0:T(1024)S(1)}, f32[768]{0:T(1024)}, u32[]{:S(2)}) copy-start(f32[768]{0:T(1024)} %get-tuple-element.450) | copy-start | bytes 9220
  1120.6 7.9 copy-start.21
  1120.6 9.3 copy-start.20
  1120.6 10.7 copy-start.1
  (41 other events, 91.4 us)
Sparse Core Ops, SparseCore 0:
  75.8 122.2 all-reduce.6
  230.1 155.0 all-gather.2
  440.9 61.3 reduce-scatter.1
  532.3 118.6 all-reduce.8
  756.8 120.0 all-reduce.10
  883.0 237.6 all-reduce.12
